TPU v7x, 32 devices: a whole 2x2x4 slice. The times are simulated.
32 devices in a mesh: fsdp: 4 (over z), tensor: 8 (over y, x, core).
Axes of the slice: x: 2, y: 2, z: 4, core: 2. Of those that a mesh axis runs over, the one named last changes fastest.
Arguments:
- tokens: bfloat16 [5120, 2048], P(('fsdp', 'tensor')), may hold values from -6 to 6
- gain_attn: bfloat16 [2048], replicated, may hold values from 0.099609375 to 1.8984375
- gain_mlp: bfloat16 [2048], replicated, may hold values from 0.099609375 to 1.8984375
- w_query: bfloat16 [2048, 2048], P('fsdp', 'tensor'), may hold values from -0.125 to 0.125
- w_key: bfloat16 [2048, 2048], P('fsdp', 'tensor'), may hold values from -0.125 to 0.125
- w_value: bfloat16 [2048, 2048], P('fsdp', 'tensor'), may hold values from -0.125 to 0.125
- w_out: bfloat16 [2048, 2048], P('tensor', 'fsdp'), may hold values from -0.5 to 0.5
- w_gate: bfloat16 [2048, 8192], P('fsdp', 'tensor'), may hold values from -0.125 to 0.125
- w_up: bfloat16 [2048, 8192], P('fsdp', 'tensor'), may hold values from -0.125 to 0.125
- w_down: bfloat16 [8192, 2048], P('tensor', 'fsdp'), may hold values from -0.09375 to 0.09375
- segment_ids: int32 [4, 1280], P('fsdp'), may hold values from 0 to 3, never falling along the last dimension, each value on 1 to 512 neighbouring positions
- out_grad: bfloat16 [5120, 2048], P(('fsdp', 'tensor')), may hold values from -6 to 6
Outputs:
- output: bfloat16 [5120, 2048], P(('fsdp', 'tensor'))
- tokens_grad: bfloat16 [5120, 2048], P(('fsdp', 'tensor'))
- gain_attn_grad: float32 [2048], replicated
- gain_mlp_grad: float32 [2048], replicated
- w_query_grad: float32 [2048, 2048], P('fsdp', 'tensor')
- w_key_grad: float32 [2048, 2048], P('fsdp', 'tensor')
- w_value_grad: float32 [2048, 2048], P('fsdp', 'tensor')
- w_out_grad: float32 [2048, 2048], P('tensor', 'fsdp')
- w_gate_grad: float32 [2048, 8192], P('fsdp', 'tensor')
- w_up_grad: float32 [2048, 8192], P('fsdp', 'tensor')
- w_down_grad: float32 [8192, 2048], P('tensor', 'fsdp')
Inputs may be any that keep to these rules, and one draw needn't show every extreme that they name: `segment_ids`: in each packed row the ids never fall; each sample has 1 to 512 tokens, and some sample in each row has exactly 512.
All inputs are finite; a program needn't handle non-finite values.
Results may differ from a plain program's by a relative error of at most 0.019.
Values may be sent and summed in bfloat16 or wider, within the bound.
A program may use at most 192 MiB of HBM per device.

v0:
```python
import math
import jax
import jax.numpy as jnp
from jax import lax
from jax.sharding import PartitionSpec as P

HEAD = 64
eps = 1e-05
rope_base = 130000.0


def dot_nt(left, right):
    return lax.dot_general(
        left, right, (((1,), (1,)), ((), ())), preferred_element_type=jnp.float32
    )


def dot_tn(left, right):
    return lax.dot_general(
        left, right, (((0,), (0,)), ((), ())), preferred_element_type=jnp.float32
    )


def rope_tables(segments):
    length = segments.shape[1]
    index = jnp.arange(length, dtype=jnp.int32)[None, :]
    change = jnp.concatenate(
        [jnp.ones((segments.shape[0], 1), dtype=bool), segments[:, 1:] != segments[:, :-1]], axis=1
    )
    start = lax.cummax(jnp.where(change, index, 0), axis=1)
    position = (index - start).astype(jnp.float32)
    half = jnp.arange(HEAD // 2, dtype=jnp.float32)
    inverse = jnp.exp(half * (-2.0 / HEAD) * math.log(rope_base))
    angle = position[:, :, None, None] * inverse[None, None, None, :]
    return (jnp.cos(angle), jnp.sin(angle))


def rotate(value, cosine, sine):
    half = value.shape[-1] // 2
    first = value[..., :half]
    second = value[..., half:]
    return jnp.concatenate(
        [first * cosine - second * sine, second * cosine + first * sine], axis=-1
    )


def norm_forward(value, gain):
    scale = lax.rsqrt(jnp.mean(value * value, axis=-1, keepdims=True) + eps)
    return (value * scale * gain, scale)


def norm_backward(value, scale, gain, grad):
    scaled_grad = grad * gain
    inner = jnp.mean(value * scaled_grad, axis=-1, keepdims=True)
    back = scale * scaled_grad - value * scale * scale * scale * inner
    gain_grad = jnp.sum(grad * value * scale, axis=0)
    return (back, gain_grad)


def row_mask(segments):
    length = segments.shape[0]
    index = jnp.arange(length, dtype=jnp.int32)
    return (segments[:, None] == segments[None, :]) & (index[None, :] <= index[:, None])


def row_scores(query, key, segments):
    scores = jnp.einsum("qhd,khd->hqk", query, key, preferred_element_type=jnp.float32) * HEAD ** (
        -0.5
    )
    return jnp.where(row_mask(segments)[None, :, :], scores, -1000000000.0)


def attend_row(inputs):
    query, key, value, segments = inputs
    scores = row_scores(query, key, segments)
    top = jnp.max(scores, axis=-1, keepdims=True)
    expo = jnp.exp(scores - top)
    total = jnp.sum(expo, axis=-1, keepdims=True)
    weights = (expo / total).astype(jnp.bfloat16)
    attended = jnp.einsum("hqk,khd->qhd", weights, value, preferred_element_type=jnp.float32)
    return (attended, (top + jnp.log(total))[..., 0])


def attend_back(inputs):
    query, key, value, segments, logsum, grad_out = inputs
    scores = row_scores(query, key, segments)
    weights = jnp.exp(scores - logsum[..., None])
    grad_value = jnp.einsum(
        "hqk,qhd->khd", weights.astype(jnp.bfloat16), grad_out, preferred_element_type=jnp.float32
    )
    grad_weights = jnp.einsum("qhd,khd->hqk", grad_out, value, preferred_element_type=jnp.float32)
    inner = jnp.sum(weights * grad_weights, axis=-1, keepdims=True)
    grad_scores = (weights * (grad_weights - inner)).astype(jnp.bfloat16)
    grad_query = jnp.einsum(
        "hqk,khd->qhd", grad_scores, key, preferred_element_type=jnp.float32
    ) * HEAD ** (-0.5)
    grad_key = jnp.einsum(
        "hqk,qhd->khd", grad_scores, query, preferred_element_type=jnp.float32
    ) * HEAD ** (-0.5)
    return (grad_query, grad_key, grad_value)


def shards(
    tokens,
    gain_attn,
    gain_mlp,
    w_query,
    w_key,
    w_value,
    w_out,
    w_gate,
    w_up,
    w_down,
    segment_ids,
    out_grad,
):
    rows_grp = segment_ids.shape[0]
    row_len = segment_ids.shape[1]
    local = (w_query, w_key, w_value, w_out, w_gate, w_up, w_down)
    gathered = (
        lax.all_gather(local[0], "fsdp", axis=0, tiled=True),
        lax.all_gather(local[1], "fsdp", axis=0, tiled=True),
        lax.all_gather(local[2], "fsdp", axis=0, tiled=True),
        lax.all_gather(local[3], "fsdp", axis=1, tiled=True),
        lax.all_gather(local[4], "fsdp", axis=0, tiled=True),
        lax.all_gather(local[5], "fsdp", axis=0, tiled=True),
        lax.all_gather(local[6], "fsdp", axis=1, tiled=True),
    )
    wq, wk, wv, wo, wg, wu, wd = gathered
    heads_dev = wq.shape[1] // HEAD
    group = rows_grp * row_len
    gain_a = gain_attn.astype(jnp.float32)
    gain_m = gain_mlp.astype(jnp.float32)
    cosine, sine = rope_tables(segment_ids)

    def heads(value):
        return value.reshape(rows_grp, row_len, heads_dev, HEAD)

    x = tokens.astype(jnp.float32)
    normed_local, scale_a = norm_forward(x, gain_a)
    normed_a = lax.all_gather(normed_local.astype(jnp.bfloat16), "tensor", axis=0, tiled=True)
    query = rotate(
        heads(jnp.dot(normed_a, wq, preferred_element_type=jnp.float32)), cosine, sine
    ).astype(jnp.bfloat16)
    key = rotate(
        heads(jnp.dot(normed_a, wk, preferred_element_type=jnp.float32)), cosine, sine
    ).astype(jnp.bfloat16)
    value = heads(jnp.dot(normed_a, wv, preferred_element_type=jnp.float32).astype(jnp.bfloat16))
    attended, logsum = lax.map(attend_row, (query, key, value, segment_ids))
    attended = attended.reshape(group, heads_dev * HEAD).astype(jnp.bfloat16)
    hidden = x + lax.psum_scatter(
        jnp.dot(attended, wo, preferred_element_type=jnp.float32),
        "tensor",
        scatter_dimension=0,
        tiled=True,
    )
    normed_hidden, scale_m = norm_forward(hidden, gain_m)
    normed_m = lax.all_gather(normed_hidden.astype(jnp.bfloat16), "tensor", axis=0, tiled=True)
    gate = jnp.dot(normed_m, wg, preferred_element_type=jnp.float32)
    up = jnp.dot(normed_m, wu, preferred_element_type=jnp.float32)
    sigma = jax.nn.sigmoid(gate)
    silu_gate = gate * sigma
    act = (silu_gate * up).astype(jnp.bfloat16)
    output = hidden + lax.psum_scatter(
        jnp.dot(act, wd, preferred_element_type=jnp.float32).astype(jnp.bfloat16),
        "tensor",
        scatter_dimension=0,
        tiled=True,
    ).astype(jnp.float32)
    wq, wk, wv, wo, wg, wu, wd = (
        lax.all_gather(local[0], "fsdp", axis=0, tiled=True),
        lax.all_gather(local[1], "fsdp", axis=0, tiled=True),
        lax.all_gather(local[2], "fsdp", axis=0, tiled=True),
        lax.all_gather(local[3], "fsdp", axis=1, tiled=True),
        lax.all_gather(local[4], "fsdp", axis=0, tiled=True),
        lax.all_gather(local[5], "fsdp", axis=0, tiled=True),
        lax.all_gather(local[6], "fsdp", axis=1, tiled=True),
    )
    grad_all = lax.all_gather(out_grad, "tensor", axis=0, tiled=True)
    grad_down = dot_tn(act, grad_all)
    grad_act = dot_nt(grad_all, wd)
    grad_gate = (grad_act * up * (sigma * (1.0 + gate * (1.0 - sigma)))).astype(jnp.bfloat16)
    grad_up = (grad_act * silu_gate).astype(jnp.bfloat16)
    grad_wgate = dot_tn(normed_m, grad_gate)
    grad_wup = dot_tn(normed_m, grad_up)
    grad_nm = lax.psum_scatter(
        dot_nt(grad_gate, wg) + dot_nt(grad_up, wu), "tensor", scatter_dimension=0, tiled=True
    )
    back_m, gain_m_part = norm_backward(hidden, scale_m, gain_m, grad_nm)
    grad_hidden = out_grad.astype(jnp.float32) + back_m
    grad_hidden_low = grad_hidden.astype(jnp.bfloat16)
    branch_all = lax.all_gather(grad_hidden_low, "tensor", axis=0, tiled=True)
    grad_wout = dot_tn(attended, branch_all)
    grad_attended = heads(dot_nt(branch_all, wo).astype(jnp.bfloat16))
    grad_query, grad_key, grad_value = lax.map(
        attend_back, (query, key, value, segment_ids, logsum, grad_attended)
    )
    grad_qpre = (
        rotate(grad_query, cosine, -sine).reshape(group, heads_dev * HEAD).astype(jnp.bfloat16)
    )
    grad_kpre = (
        rotate(grad_key, cosine, -sine).reshape(group, heads_dev * HEAD).astype(jnp.bfloat16)
    )
    grad_vpre = grad_value.reshape(group, heads_dev * HEAD).astype(jnp.bfloat16)
    grad_wq = dot_tn(normed_a, grad_qpre)
    grad_wk = dot_tn(normed_a, grad_kpre)
    grad_wv = dot_tn(normed_a, grad_vpre)
    grad_na_part = dot_nt(grad_qpre, wq) + dot_nt(grad_kpre, wk) + dot_nt(grad_vpre, wv)
    grad_na = lax.psum_scatter(
        grad_na_part.astype(jnp.bfloat16), "tensor", scatter_dimension=0, tiled=True
    ).astype(jnp.float32)
    back_a, gain_a_part = norm_backward(x, scale_a, gain_a, grad_na)
    tokens_grad = (grad_hidden + back_a).astype(jnp.bfloat16)
    gain_a_grad, gain_m_grad = lax.psum((gain_a_part, gain_m_part), ("fsdp", "tensor"))
    weight_grads = (
        lax.psum_scatter(
            grad_wq.astype(jnp.bfloat16), "fsdp", scatter_dimension=0, tiled=True
        ).astype(jnp.float32),
        lax.psum_scatter(
            grad_wk.astype(jnp.bfloat16), "fsdp", scatter_dimension=0, tiled=True
        ).astype(jnp.float32),
        lax.psum_scatter(
            grad_wv.astype(jnp.bfloat16), "fsdp", scatter_dimension=0, tiled=True
        ).astype(jnp.float32),
        lax.psum_scatter(
            grad_wout.astype(jnp.bfloat16), "fsdp", scatter_dimension=1, tiled=True
        ).astype(jnp.float32),
        lax.psum_scatter(
            grad_wgate.astype(jnp.bfloat16), "fsdp", scatter_dimension=0, tiled=True
        ).astype(jnp.float32),
        lax.psum_scatter(
            grad_wup.astype(jnp.bfloat16), "fsdp", scatter_dimension=0, tiled=True
        ).astype(jnp.float32),
        lax.psum_scatter(
            grad_down.astype(jnp.bfloat16), "fsdp", scatter_dimension=1, tiled=True
        ).astype(jnp.float32),
    )
    return (
        output.astype(jnp.bfloat16),
        tokens_grad,
        gain_a_grad,
        gain_m_grad,
        weight_grads[0],
        weight_grads[1],
        weight_grads[2],
        weight_grads[3],
        weight_grads[4],
        weight_grads[5],
        weight_grads[6],
    )


def solution(mesh):
    return jax.shard_map(
        shards,
        mesh=mesh,
        in_specs=(
            P(("fsdp", "tensor"), None),
            P(),
            P(),
            P("fsdp", "tensor"),
            P("fsdp", "tensor"),
            P("fsdp", "tensor"),
            P("tensor", "fsdp"),
            P("fsdp", "tensor"),
            P("fsdp", "tensor"),
            P("tensor", "fsdp"),
            P("fsdp", None),
            P(("fsdp", "tensor"), None),
        ),
        out_specs=(
            P(("fsdp", "tensor"), None),
            P(("fsdp", "tensor"), None),
            P(),
            P(),
            P("fsdp", "tensor"),
            P("fsdp", "tensor"),
            P("fsdp", "tensor"),
            P("tensor", "fsdp"),
            P("fsdp", "tensor"),
            P("fsdp", "tensor"),
            P("tensor", "fsdp"),
        ),
        check_vma=False,
    )
```

profile of v0, /device:TPU:0, one launch (start us, length us, event | category | flops | bytes accessed | tf_op | source)
XLA Modules:
  0.0 1231.1 jit_solution(9686080261791631921)
XLA Ops:
  20.3 20.0 %all-gather.18.cloned.1.call-done = bf16[2048,256]{1,0:T(8,128)(2,1)} async-done(((bf16[512,256]{1,0:T(8,128)(2,1)}), bf16[2048,256]{1,0:T(8,128)(2,1)}) %all-gather.18.cloned.1.call-update) | async-done | bytes 1048592 | tf_op jit(solution)/shard_map/all_gather | solution.py:122
  40.3 43.0 %all-gather.12.cloned.1.call-done = bf16[1280,2048]{1,0:T(8,128)(2,1)} async-done(((bf16[160,2048]{1,0:T(8,128)(2,1)}), bf16[1280,2048]{1,0:T(8,128)(2,1)}) %all-gather.12.cloned.1.call-update) | async-done | bytes 5242896 | tf_op jit(solution)/shard_map/all_gather | solution.py:141
  87.7 25.2 %all-gather.16.cloned.1.call-done = bf16[2048,256]{1,0:T(8,128)(2,1)} async-done(((bf16[512,256]{1,0:T(8,128)(2,1)}), bf16[2048,256]{1,0:T(8,128)(2,1)}) %all-gather.16.cloned.1.call-update) | async-done | bytes 1048592 | tf_op jit(solution)/shard_map/all_gather | solution.py:121
  117.6 11.1 fusion.39
  146.1 21.8 %fusion.14 = bf16[4,64,1280]{2,1,0:T(8,128)(2,1)S(1)} fusion(bf16[1280,4,64]{0,2,1:T(8,128)(2,1)S(1)} %bitcast.97, f32[4,1280,1280]{1,2,0:T(8,128)} %get-tuple-element.91, f32[4,1280]{1,0:T(4,128)S(1)} %fusion.1, f32[4,1280]{1,0:T(4,128)S(1)} %get-tuple-element.90), kind=kOutput, calls=%fused_computation.41 | convolution fusion | flops 858849280 | bytes 27566080 | tf_op jit(solution)/shard_map/while/body/eval_jaxpr/hqk,khd->qhd/dot_general | solution.py:80
  178.2 80.4 %reduce-scatter.12.cloned.1.call-done = f32[160,2048]{1,0:T(8,128)} async-done(((f32[1280,2048]{1,0:T(8,128)}), f32[160,2048]{1,0:T(8,128)}) %reduce-scatter.12.cloned.1.call-update) | async-done | bytes 1310736 | tf_op jit(solution)/shard_map/reduce_scatter | solution.py:151
  263.3 77.6 %all-gather.26.cloned.1.call-done = bf16[2048,1024]{1,0:T(8,128)(2,1)} async-done(((bf16[512,1024]{1,0:T(8,128)(2,1)}), bf16[2048,1024]{1,0:T(8,128)(2,1)}) %all-gather.26.cloned.1.call-update) | async-done | bytes 4194320 | tf_op jit(solution)/shard_map/all_gather | solution.py:126
  340.9 42.1 %all-gather.22.cloned.1.call-done = bf16[1280,2048]{1,0:T(8,128)(2,1)} async-done(((bf16[160,2048]{1,0:T(8,128)(2,1)}), bf16[1280,2048]{1,0:T(8,128)(2,1)}) %all-gather.22.cloned.1.call-update) | async-done | bytes 5242896 | tf_op jit(solution)/shard_map/all_gather | solution.py:158
  393.3 72.2 %all-gather.24.cloned.1.call-done = bf16[2048,1024]{1,0:T(8,128)(2,1)} async-done(((bf16[512,1024]{1,0:T(8,128)(2,1)}), bf16[2048,1024]{1,0:T(8,128)(2,1)}) %all-gather.24.cloned.1.call-update) | async-done | bytes 4194320 | tf_op jit(solution)/shard_map/all_gather | solution.py:125
  475.6 70.5 %all-gather.28.cloned.1.call-done = bf16[1024,2048]{1,0:T(8,128)(2,1)} async-done(((bf16[1024,512]{1,0:T(8,128)(2,1)}), bf16[1024,2048]{1,0:T(8,128)(2,1)}) %all-gather.28.cloned.1.call-update) | async-done | bytes 4194320 | tf_op jit(solution)/shard_map/all_gather | solution.py:127
  546.2 41.6 %all-gather.30.cloned.1.call-done = bf16[1280,2048]{1,0:T(8,128)(2,1)} async-done(((bf16[160,2048]{1,0:T(8,128)(2,1)}), bf16[1280,2048]{1,0:T(8,128)(2,1)}) %all-gather.30.cloned.1.call-update) | async-done | bytes 5242896 | tf_op jit(solution)/shard_map/all_gather | solution.py:179
  587.7 14.7 %multiply_convert_fusion.1 = (bf16[1280,1024]{1,0:T(8,128)(2,1)S(1)}, bf16[1280,1024]{1,0:T(8,128)(2,1)S(1)}, bf16[1280,1024]{1,0:T(8,128)(2,1)}) fusion(f32[1280,1024]{1,0:T(8,128)} %fusion.43, f32[1280,1024]{1,0:T(8,128)} %fusion.44, bf16[1280,2048]{1,0:T(8,128)(2,1)} %all-gather.30.cloned.1.call-done, bf16[1024,2048]{1,0:T(8,128)(2,1)} %all-gather.28.cloned.1.call-done), kind=kOutput, calls=%fused_computation.17 | convolution fusion | flops 5388369920 | bytes 27787264 | tf_op jit(solution)/shard_map/dot_general | solution.py:13
  621.7 81.7 %reduce-scatter.16.cloned.1.call-done = f32[160,2048]{1,0:T(8,128)} async-done(((f32[1280,2048]{1,0:T(8,128)}), f32[160,2048]{1,0:T(8,128)}) %reduce-scatter.16.cloned.1.call-update) | async-done | bytes 1310736 | tf_op jit(solution)/shard_map/reduce_scatter | solution.py:186
  774.3 16.7 %multiply_reduce_fusion = (f32[4,1280]{1,0:T(4,128)S(1)}, f32[4,1280,1280]{1,2,0:T(8,128)}) fusion(f32[4,1280,1280]{1,2,0:T(8,128)} %get-tuple-element.91, f32[4,1280]{1,0:T(4,128)S(1)} %log_add_fusion, bf16[1280,4,64]{0,2,1:T(8,128)(2,1)S(1)} %bitcast.90, bf16[1280,4,64]{0,2,1:T(8,128)(2,1)S(1)} %bitcast.98), kind=kOutput, calls=%fused_computation.3 | convolution fusion | flops 858516480 | bytes 53780480 | tf_op jit(solution)/shard_map/while/body/eval_jaxpr/qhd,khd->hqk/dot_general | solution.py:91
  791.2 22.5 %multiply_convert_fusion = bf16[4,1280,1280]{1,2,0:T(8,128)(2,1)} fusion(f32[4,1280,1280]{1,2,0:T(8,128)} %get-tuple-element.93, f32[4,1280,1280]{1,2,0:T(8,128)} %get-tuple-element.91, f32[4,1280]{1,0:T(4,128)S(1)} %get-tuple-element.92, f32[4,1280]{1,0:T(4,128)S(1)} %log_add_fusion), kind=kLoop, calls=%fused_computation.2 | loop fusion | flops 26214400 | bytes 65576960 | tf_op jit(solution)/shard_map/while/body/eval_jaxpr/convert_element_type | solution.py:93
  868.5 39.0 %reduce-scatter.30.cloned.1.call-done = bf16[512,1024]{1,0:T(8,128)(2,1)} async-done(((bf16[2048,1024]{1,0:T(8,128)(2,1)}), bf16[512,1024]{1,0:T(8,128)(2,1)}) %reduce-scatter.30.cloned.1.call-update) | async-done | bytes 1048592 | tf_op jit(solution)/shard_map/reduce_scatter | solution.py:231
  910.3 76.6 %reduce-scatter.28.cloned.1.call-done = bf16[512,1024]{1,0:T(8,128)(2,1)} async-done(((bf16[2048,1024]{1,0:T(8,128)(2,1)}), bf16[512,1024]{1,0:T(8,128)(2,1)}) %reduce-scatter.28.cloned.1.call-update) | async-done | bytes 1048592 | tf_op jit(solution)/shard_map/reduce_scatter | solution.py:228
  989.7 27.2 %reduce-scatter.26.cloned.1.call-done = bf16[256,512]{1,0:T(8,128)(2,1)} async-done(((bf16[256,2048]{1,0:T(8,128)(2,1)}), bf16[256,512]{1,0:T(8,128)(2,1)}) %reduce-scatter.26.cloned.1.call-update) | async-done | bytes 262160 | tf_op jit(solution)/shard_map/reduce_scatter | solution.py:225
  1018.7 26.1 %reduce-scatter.24.cloned.1.call-done = bf16[512,256]{1,0:T(8,128)(2,1)} async-done(((bf16[2048,256]{1,0:T(8,128)(2,1)}), bf16[512,256]{1,0:T(8,128)(2,1)}) %reduce-scatter.24.cloned.1.call-update) | async-done | bytes 262160 | tf_op jit(solution)/shard_map/reduce_scatter | solution.py:222
  1046.6 26.5 %reduce-scatter.22.cloned.1.call-done = bf16[512,256]{1,0:T(8,128)(2,1)} async-done(((bf16[2048,256]{1,0:T(8,128)(2,1)}), bf16[512,256]{1,0:T(8,128)(2,1)}) %reduce-scatter.22.cloned.1.call-update) | async-done | bytes 262160 | tf_op jit(solution)/shard_map/reduce_scatter | solution.py:219
  1074.9 26.2 %reduce-scatter.20.cloned.1.call-done = bf16[512,256]{1,0:T(8,128)(2,1)} async-done(((bf16[2048,256]{1,0:T(8,128)(2,1)}), bf16[512,256]{1,0:T(8,128)(2,1)}) %reduce-scatter.20.cloned.1.call-update) | async-done | bytes 262160 | tf_op jit(solution)/shard_map/reduce_scatter | solution.py:216
  1102.8 57.3 %reduce-scatter.18.cloned.1.call-done = bf16[160,2048]{1,0:T(8,128)(2,1)} async-done(((bf16[1280,2048]{1,0:T(8,128)(2,1)}), bf16[160,2048]{1,0:T(8,128)(2,1)}) %reduce-scatter.18.cloned.1.call-update) | async-done | bytes 655376 | tf_op jit(solution)/shard_map/reduce_scatter | solution.py:209
  1161.6 39.8 %all-reduce = (f32[2048]{0:T(1024)}, f32[2048]{0:T(1024)}) all-reduce(f32[2048]{0:T(1024)S(1)} %get-tuple-element.54, f32[2048]{0:T(1024)S(1)} %get-tuple-element.52), channel_id=1, replica_groups=mesh['fsdp'=4,'tensor'=8] {'fsdp','tensor'}, use_global_device_ids=true, to_apply=%region_14.15 | all-reduce | flops 4096 | bytes 32768 | tf_op jit(solution)/shard_map/psum | solution.py:214
  1201.4 19.3 %reduce-scatter.14.cloned.1.call-done = bf16[160,2048]{1,0:T(8,128)(2,1)} async-done(((bf16[1280,2048]{1,0:T(8,128)(2,1)}), bf16[160,2048]{1,0:T(8,128)(2,1)}) %reduce-scatter.14.cloned.1.call-update) | async-done | bytes 655376 | tf_op jit(solution)/shard_map/reduce_scatter | solution.py:164
  (167 shorter events, 237.3 us)
Async XLA Ops:
  7.2 33.1 %all-gather.18.cloned.1.call-start = ((), (), s32[]{:S(2)}) async-start(), calls=%async_computation.14 | async-start | bytes 1310720 | tf_op jit(solution)/shard_map/all_gather | solution.py:122
  7.9 75.4 %all-gather.12.cloned.1.call-start = ((), (), s32[]{:S(2)}) async-start(), calls=%async_computation.11 | async-start | bytes 5898240 | tf_op jit(solution)/shard_map/all_gather | solution.py:141
  12.7 100.2 %all-gather.16.cloned.1.call-start = ((), (), s32[]{:S(2)}) async-start(), calls=%async_computation.13 | async-start | bytes 1310720 | tf_op jit(solution)/shard_map/all_gather | solution.py:121
  13.4 128.3 %all-gather.14.cloned.1.call-start = ((), (), s32[]{:S(2)}) async-start(), calls=%async_computation.12 | async-start | bytes 1310720 | tf_op jit(solution)/shard_map/all_gather | solution.py:123
  14.0 156.6 %all-gather.20.cloned.1.call-start = ((), (), s32[]{:S(2)}) async-start(), calls=%async_computation.15 | async-start | bytes 1310720 | tf_op jit(solution)/shard_map/all_gather | solution.py:124
  14.6 243.9 %reduce-scatter.12.cloned.1.call-start = ((), (), s32[]{:S(2)}) async-start(), calls=%async_computation.16 | async-start | bytes 11796480 | tf_op jit(solution)/shard_map/reduce_scatter | solution.py:151
  177.4 163.5 %all-gather.26.cloned.1.call-start = ((), (), s32[]{:S(2)}) async-start(), calls=%async_computation.19 | async-start | bytes 5242880 | tf_op jit(solution)/shard_map/all_gather | solution.py:126
  178.1 204.9 %all-gather.22.cloned.1.call-start = ((), (), s32[]{:S(2)}) async-start(), calls=%async_computation.17 | async-start | bytes 5898240 | tf_op jit(solution)/shard_map/all_gather | solution.py:158
  261.2 204.2 %all-gather.24.cloned.1.call-start = ((), (), s32[]{:S(2)}) async-start(), calls=%async_computation.18 | async-start | bytes 5242880 | tf_op jit(solution)/shard_map/all_gather | solution.py:125
  261.9 284.2 %all-gather.28.cloned.1.call-start = ((), (), s32[]{:S(2)}) async-start(), calls=%async_computation.20 | async-start | bytes 5242880 | tf_op jit(solution)/shard_map/all_gather | solution.py:127
  262.5 325.2 %all-gather.30.cloned.1.call-start = ((), (), s32[]{:S(2)}) async-start(), calls=%async_computation.22 | async-start | bytes 5898240 | tf_op jit(solution)/shard_map/all_gather | solution.py:179
  263.2 440.2 %reduce-scatter.16.cloned.1.call-start = ((), (), s32[]{:S(2)}) async-start(), calls=%async_computation.23 | async-start | bytes 11796480 | tf_op jit(solution)/shard_map/reduce_scatter | solution.py:186
  621.7 127.3 %all-gather.32.cloned.1.call-start = ((), (), s32[]{:S(2)}) async-start(), calls=%async_computation.24 | async-start | bytes 5898240 | tf_op jit(solution)/shard_map/all_gather | solution.py:192
  707.8 157.9 %reduce-scatter.32.cloned.1.call-start = ((), (), s32[]{:S(2)}) async-start(), calls=%async_computation.32 | async-start | bytes 5242880 | tf_op jit(solution)/shard_map/reduce_scatter | solution.py:234
  717.9 189.6 %reduce-scatter.30.cloned.1.call-start = ((), (), s32[]{:S(2)}) async-start(), calls=%async_computation.31 | async-start | bytes 5242880 | tf_op jit(solution)/shard_map/reduce_scatter | solution.py:231
  728.2 258.8 %reduce-scatter.28.cloned.1.call-start = ((), (), s32[]{:S(2)}) async-start(), calls=%async_computation.30 | async-start | bytes 5242880 | tf_op jit(solution)/shard_map/reduce_scatter | solution.py:228
  738.4 278.4 %reduce-scatter.26.cloned.1.call-start = ((), (), s32[]{:S(2)}) async-start(), calls=%async_computation.29 | async-start | bytes 1310720 | tf_op jit(solution)/shard_map/reduce_scatter | solution.py:225
  754.0 290.8 %reduce-scatter.24.cloned.1.call-start = ((), (), s32[]{:S(2)}) async-start(), calls=%async_computation.28 | async-start | bytes 1310720 | tf_op jit(solution)/shard_map/reduce_scatter | solution.py:222
  791.0 282.1 %reduce-scatter.22.cloned.1.call-start = ((), (), s32[]{:S(2)}) async-start(), calls=%async_computation.27 | async-start | bytes 1310720 | tf_op jit(solution)/shard_map/reduce_scatter | solution.py:219
  833.1 267.9 %reduce-scatter.20.cloned.1.call-start = ((), (), s32[]{:S(2)}) async-start(), calls=%async_computation.26 | async-start | bytes 1310720 | tf_op jit(solution)/shard_map/reduce_scatter | solution.py:216
  838.3 321.8 %reduce-scatter.18.cloned.1.call-start = ((), (), s32[]{:S(2)}) async-start(), calls=%async_computation.25 | async-start | bytes 5898240 | tf_op jit(solution)/shard_map/reduce_scatter | solution.py:209
  855.5 365.1 %reduce-scatter.14.cloned.1.call-start = ((), (), s32[]{:S(2)}) async-start(), calls=%async_computation.21 | async-start | bytes 5898240 | tf_op jit(solution)/shard_map/reduce_scatter | solution.py:164
  868.5 291.6 %copy-start.20 = (f32[160]{0:T(256)S(1)}, f32[160]{0:T(256)}, u32[]{:S(2)}) copy-start(f32[160]{0:T(256)} %copy-done.19) | copy-start | bytes 1924
  910.3 310.4 %copy-start.2 = (f32[160,2048]{1,0:T(8,128)S(1)}, f32[160,2048]{1,0:T(8,128)}, u32[]{:S(2)}) copy-start(f32[160,2048]{1,0:T(8,128)} %reduce-scatter.16.cloned.1.call-done) | copy-start | bytes 3932164
  (26 other events, 1042.0 us)
Sparse Core Ops, SparseCore 0:
  9.6 30.6 all-gather.17
  42.8 40.5 all-gather.11
  84.9 27.9 all-gather.15
  114.3 27.4 all-gather.13
  143.2 27.4 all-gather.19
  177.5 81.0 reduce-scatter.11
  260.1 80.7 all-gather.25
  343.4 39.6 all-gather.21
  384.6 80.7 all-gather.23
  466.8 79.2 all-gather.27
  548.0 39.6 all-gather.29
  621.8 81.5 reduce-scatter.15
  707.9 41.0 all-gather.31
  751.2 76.7 reduce-scatter.31
  830.2 77.2 reduce-scatter.29
  909.7 77.2 reduce-scatter.27
  989.2 27.6 reduce-scatter.25
  1019.0 25.7 reduce-scatter.23
  1047.2 25.8 reduce-scatter.21
  1075.2 25.7 reduce-scatter.19
  1104.8 55.2 reduce-scatter.17
  1163.5 57.1 reduce-scatter.13
where the time goes:
time: 1240 us; the launch traced here: 1230 us
  waiting for transfers between devices  873 us (70%)
  matrix products  230 us (19%)
  other arithmetic  70.7 us (6%)
  blocking collectives  39.8 us (3%)
  between operations  15 us (1%)
    reduce_scatter x1, waiting for transfers between devices, shards(): lax.psum_scatter(dot_nt(grad_gate, wg) + dot_nt(grad_up, wu), 'tensor', s...  81.7 us
    reduce_scatter x1, waiting for transfers between devices, shards(): lax.psum_scatter(jnp.dot(attended, wo, preferred_element_type=jnp.float32...  80.4 us
    all_gather x1, waiting for transfers between devices, shards(): lax.all_gather(local[5], 'fsdp', axis=0, tiled=True)  77.6 us
    reduce_scatter x1, waiting for transfers between devices, shards(): lax.psum_scatter(grad_wgate.astype(jnp.bfloat16), 'fsdp', scatter_dimensi...  76.6 us
    all_gather x1, waiting for transfers between devices, shards(): lax.all_gather(local[4], 'fsdp', axis=0, tiled=True)  72.2 us
    all_gather x1, waiting for transfers between devices, shards(): lax.all_gather(local[6], 'fsdp', axis=1, tiled=True)  70.5 us
    reduce_scatter x1, waiting for transfers between devices, shards(): lax.psum_scatter(grad_na_part.astype(jnp.bfloat16), 'tensor', scatter_dim...  57.3 us
    dot_general x7, matrix products, dot_nt(): lax.dot_general(left, right, (((1,), (1,)), ((), ())), preferred_element_...  55.2 us
  transfers between devices with their start and end apart: 22, of which 21 were waited for; matrix products, arithmetic and copies ran while one was open for 21% of the time, Pallas kernels for 0%

commit v1 on v0

--- a/solution.py
+++ b/solution.py
@@ -7,6 +7,32 @@
 HEAD = 64
 eps = 1e-05
 rope_base = 130000.0
+
+
+def _create_circles(w_in, ndim_at):
+    g_now = list(w_in.shape[1:])
+    g_now[ndim_at] *= w_in.shape[0]
+    value_now = jnp.moveaxis(w_in, 0, ndim_at).reshape(g_now)
+    return value_now
+
+
+def press_numbers_here(page, peer_axis):
+    long_array = page[None]
+    n = jax.lax.psum(1, peer_axis)
+    for k0 in range(n.bit_length() - 1):
+        p_next = 1 << k0
+        main = jax.lax.ppermute(
+            long_array, peer_axis, list(map(lambda p: (p, p ^ p_next), range(n)))
+        )
+        x_new = jnp.stack([long_array, main], axis=0)
+        plain = jax.lax.axis_index(peer_axis) >> k0 & 1
+        long_array = jnp.where(plain == 0, x_new, x_new[::-1]).reshape(-1, *page.shape)
+    return long_array
+
+
+def tell_fields_here(vec, z, k_dim):
+    r2 = _create_circles(press_numbers_here(vec, z), k_dim)
+    return r2
 
 
 def dot_nt(left, right):
@@ -176,7 +202,7 @@
         lax.all_gather(local[5], "fsdp", axis=0, tiled=True),
         lax.all_gather(local[6], "fsdp", axis=1, tiled=True),
     )
-    grad_all = lax.all_gather(out_grad, "tensor", axis=0, tiled=True)
+    grad_all = tell_fields_here(out_grad, "tensor", 0)
     grad_down = dot_tn(act, grad_all)
     grad_act = dot_nt(grad_all, wd)
     grad_gate = (grad_act * up * (sigma * (1.0 + gate * (1.0 - sigma)))).astype(jnp.bfloat16)

time: 1240 us -> 1200 us (0.968)
  waiting for transfers between devices: 873 us -> 830 us
  other arithmetic: 70.7 us -> 83.7 us
    ppermute x0 -> x3, waiting for transfers between devices: none -> 95.9 us  [press_numbers_here(): jax.lax.ppermute(long_array, peer_axis, list(map(lambda p: (p, p ^ p_next...]
    all_gather x1, waiting for transfers between devices: 77.6 us -> 0.01 us  [shards(): lax.all_gather(local[5], 'fsdp', axis=0, tiled=True)]
    all_gather x1 -> x0, waiting for transfers between devices: 41.6 us -> none  [shards(): grad_all = lax.all_gather(out_grad, 'tensor', axis=0, tiled=True)]
    all_gather x1, waiting for transfers between devices: 42.1 us -> 15.6 us  [shards(): lax.all_gather(normed_hidden.astype(jnp.bfloat16), 'tensor', axis=0, tile...]
  transfers between devices with their start and end apart: 22 -> 24, of which waited for: 21 -> 22; matrix products, arithmetic and copies ran while one was open for 21% -> 21% of each run, Pallas kernels for 0% -> 0%
where the time goes in v1:
time: 1200 us; the launch traced here: 1190 us
  waiting for transfers between devices  830 us (69%)
  matrix products  220 us (18%)
  other arithmetic  83.7 us (7%)
  blocking collectives  39.8 us (3%)
  between operations  15.1 us (1%)
    ppermute x3, waiting for transfers between devices, press_numbers_here(): jax.lax.ppermute(long_array, peer_axis, list(map(lambda p: (p, p ^ p_next...  95.9 us
    reduce_scatter x1, waiting for transfers between devices, shards(): lax.psum_scatter(jnp.dot(attended, wo, preferred_element_type=jnp.float32...  80.4 us
    reduce_scatter x1, waiting for transfers between devices, shards(): lax.psum_scatter(dot_nt(grad_gate, wg) + dot_nt(grad_up, wu), 'tensor', s...  80.2 us
    reduce_scatter x1, waiting for transfers between devices, shards(): lax.psum_scatter(grad_wgate.astype(jnp.bfloat16), 'fsdp', scatter_dimensi...  76.6 us
    all_gather x1, waiting for transfers between devices, shards(): lax.all_gather(local[4], 'fsdp', axis=0, tiled=True)  72 us
    all_gather x1, waiting for transfers between devices, shards(): lax.all_gather(local[6], 'fsdp', axis=1, tiled=True)  70.5 us
    reduce_scatter x1, waiting for transfers between devices, shards(): lax.psum_scatter(grad_na_part.astype(jnp.bfloat16), 'tensor', scatter_dim...  57.1 us
    dot_general x7, matrix products, dot_nt(): lax.dot_general(left, right, (((1,), (1,)), ((), ())), preferred_element_...  54.7 us
  transfers between devices with their start and end apart: 24, of which 22 were waited for; matrix products, arithmetic and copies ran while one was open for 21% of the time, Pallas kernels for 0%

profile of v1, /device:TPU:0, one launch (start us, length us, event | category | flops | bytes accessed | tf_op | source)
XLA Modules:
  0.0 1194.2 jit_solution(18056322508795903038)
XLA Ops:
  20.3 20.0 %all-gather.17.cloned.1.call-done = bf16[2048,256]{1,0:T(8,128)(2,1)} async-done(((bf16[512,256]{1,0:T(8,128)(2,1)}), bf16[2048,256]{1,0:T(8,128)(2,1)}) %all-gather.17.cloned.1.call-update) | async-done | bytes 1048592 | tf_op jit(solution)/shard_map/all_gather | solution.py:148
  40.3 43.0 %all-gather.11.cloned.1.call-done = bf16[1280,2048]{1,0:T(8,128)(2,1)} async-done(((bf16[160,2048]{1,0:T(8,128)(2,1)}), bf16[1280,2048]{1,0:T(8,128)(2,1)}) %all-gather.11.cloned.1.call-update) | async-done | bytes 5242896 | tf_op jit(solution)/shard_map/all_gather | solution.py:167
  87.7 25.2 %all-gather.15.cloned.1.call-done = bf16[2048,256]{1,0:T(8,128)(2,1)} async-done(((bf16[512,256]{1,0:T(8,128)(2,1)}), bf16[2048,256]{1,0:T(8,128)(2,1)}) %all-gather.15.cloned.1.call-update) | async-done | bytes 1048592 | tf_op jit(solution)/shard_map/all_gather | solution.py:147
  147.0 11.7 fusion.14
  158.7 12.0 %all-gather.19.cloned.1.call-done = bf16[256,2048]{1,0:T(8,128)(2,1)} async-done(((bf16[256,512]{1,0:T(8,128)(2,1)}), bf16[256,2048]{1,0:T(8,128)(2,1)}) %all-gather.19.cloned.1.call-update) | async-done | bytes 1048592 | tf_op jit(solution)/shard_map/all_gather | solution.py:150
  178.2 80.4 %reduce-scatter.12.cloned.1.call-done = f32[160,2048]{1,0:T(8,128)} async-done(((f32[1280,2048]{1,0:T(8,128)}), f32[160,2048]{1,0:T(8,128)}) %reduce-scatter.12.cloned.1.call-update) | async-done | bytes 1310736 | tf_op jit(solution)/shard_map/reduce_scatter | solution.py:177
  267.6 29.7 %collective-permute-done.1 = bf16[2,160,2048]{2,1,0:T(8,128)(2,1)} collective-permute-done((bf16[2,160,2048]{2,1,0:T(8,128)(2,1)}, bf16[2,160,2048]{2,1,0:T(8,128)(2,1)}, u32[]{:S(2)}, u32[]{:S(2)}) %collective-permute-start.1) | collective-permute-done | bytes 1310752 | tf_op jit(solution)/shard_map/ppermute | solution.py:24
  302.8 64.1 %collective-permute-done.2 = bf16[4,160,2048]{2,1,0:T(8,128)(2,1)} collective-permute-done((bf16[4,160,2048]{2,1,0:T(8,128)(2,1)}, bf16[4,160,2048]{2,1,0:T(8,128)(2,1)}, u32[]{:S(2)}, u32[]{:S(2)}) %collective-permute-start.2) | collective-permute-done | bytes 2621472 | tf_op jit(solution)/shard_map/ppermute | solution.py:24
  373.7 15.6 %all-gather.21.cloned.1.call-done = bf16[1280,2048]{1,0:T(8,128)(2,1)} async-done(((bf16[160,2048]{1,0:T(8,128)(2,1)}), bf16[1280,2048]{1,0:T(8,128)(2,1)}) %all-gather.21.cloned.1.call-update) | async-done | bytes 5242896 | tf_op jit(solution)/shard_map/all_gather | solution.py:184
  399.7 72.0 %all-gather.23.cloned.1.call-done = bf16[2048,1024]{1,0:T(8,128)(2,1)} async-done(((bf16[512,1024]{1,0:T(8,128)(2,1)}), bf16[2048,1024]{1,0:T(8,128)(2,1)}) %all-gather.23.cloned.1.call-update) | async-done | bytes 4194320 | tf_op jit(solution)/shard_map/all_gather | solution.py:151
  481.9 70.5 %all-gather.27.cloned.1.call-done = bf16[1024,2048]{1,0:T(8,128)(2,1)} async-done(((bf16[1024,512]{1,0:T(8,128)(2,1)}), bf16[1024,2048]{1,0:T(8,128)(2,1)}) %all-gather.27.cloned.1.call-update) | async-done | bytes 4194320 | tf_op jit(solution)/shard_map/all_gather | solution.py:153
  552.4 14.6 %multiply_convert_fusion.1 = (bf16[1280,1024]{1,0:T(8,128)(2,1)S(1)}, bf16[1280,1024]{1,0:T(8,128)(2,1)S(1)}, bf16[1280,1024]{1,0:T(8,128)(2,1)}) fusion(f32[1280,1024]{1,0:T(8,128)} %fusion.45, f32[1280,1024]{1,0:T(8,128)} %fusion.46, bf16[1280,2048]{1,0:T(8,128)(2,1)} %bitcast.103, bf16[1024,2048]{1,0:T(8,128)(2,1)} %all-gather.27.cloned.1.call-done), kind=kOutput, calls=%fused_computation.19 | convolution fusion | flops 5388369920 | bytes 27787264 | tf_op jit(solution)/shard_map/dot_general | solution.py:39
  586.3 80.2 %reduce-scatter.16.cloned.1.call-done = f32[160,2048]{1,0:T(8,128)} async-done(((f32[1280,2048]{1,0:T(8,128)}), f32[160,2048]{1,0:T(8,128)}) %reduce-scatter.16.cloned.1.call-update) | async-done | bytes 1310736 | tf_op jit(solution)/shard_map/reduce_scatter | solution.py:212
  737.1 16.7 %multiply_reduce_fusion = (f32[4,1280]{1,0:T(4,128)S(1)}, f32[4,1280,1280]{1,2,0:T(8,128)}) fusion(f32[4,1280,1280]{1,2,0:T(8,128)} %get-tuple-element.93, f32[4,1280]{1,0:T(4,128)S(1)} %log_add_fusion, bf16[1280,4,64]{0,2,1:T(8,128)(2,1)S(1)} %bitcast.106, bf16[1280,4,64]{0,2,1:T(8,128)(2,1)S(1)} %bitcast.114), kind=kOutput, calls=%fused_computation.3 | convolution fusion | flops 858516480 | bytes 53780480 | tf_op jit(solution)/shard_map/while/body/eval_jaxpr/qhd,khd->hqk/dot_general | solution.py:117
  754.1 22.5 %multiply_convert_fusion = bf16[4,1280,1280]{1,2,0:T(8,128)(2,1)} fusion(f32[4,1280,1280]{1,2,0:T(8,128)} %get-tuple-element.95, f32[4,1280,1280]{1,2,0:T(8,128)} %get-tuple-element.93, f32[4,1280]{1,0:T(4,128)S(1)} %get-tuple-element.94, f32[4,1280]{1,0:T(4,128)S(1)} %log_add_fusion), kind=kLoop, calls=%fused_computation.2 | loop fusion | flops 26214400 | bytes 65576960 | tf_op jit(solution)/shard_map/while/body/eval_jaxpr/convert_element_type | solution.py:119
  831.2 39.5 %reduce-scatter.30.cloned.1.call-done = bf16[512,1024]{1,0:T(8,128)(2,1)} async-done(((bf16[2048,1024]{1,0:T(8,128)(2,1)}), bf16[512,1024]{1,0:T(8,128)(2,1)}) %reduce-scatter.30.cloned.1.call-update) | async-done | bytes 1048592 | tf_op jit(solution)/shard_map/reduce_scatter | solution.py:257
  873.5 76.6 %reduce-scatter.28.cloned.1.call-done = bf16[512,1024]{1,0:T(8,128)(2,1)} async-done(((bf16[2048,1024]{1,0:T(8,128)(2,1)}), bf16[512,1024]{1,0:T(8,128)(2,1)}) %reduce-scatter.28.cloned.1.call-update) | async-done | bytes 1048592 | tf_op jit(solution)/shard_map/reduce_scatter | solution.py:254
  953.0 27.2 %reduce-scatter.26.cloned.1.call-done = bf16[256,512]{1,0:T(8,128)(2,1)} async-done(((bf16[256,2048]{1,0:T(8,128)(2,1)}), bf16[256,512]{1,0:T(8,128)(2,1)}) %reduce-scatter.26.cloned.1.call-update) | async-done | bytes 262160 | tf_op jit(solution)/shard_map/reduce_scatter | solution.py:251
  981.9 26.1 %reduce-scatter.24.cloned.1.call-done = bf16[512,256]{1,0:T(8,128)(2,1)} async-done(((bf16[2048,256]{1,0:T(8,128)(2,1)}), bf16[512,256]{1,0:T(8,128)(2,1)}) %reduce-scatter.24.cloned.1.call-update) | async-done | bytes 262160 | tf_op jit(solution)/shard_map/reduce_scatter | solution.py:248
  1009.9 26.3 %reduce-scatter.22.cloned.1.call-done = bf16[512,256]{1,0:T(8,128)(2,1)} async-done(((bf16[2048,256]{1,0:T(8,128)(2,1)}), bf16[512,256]{1,0:T(8,128)(2,1)}) %reduce-scatter.22.cloned.1.call-update) | async-done | bytes 262160 | tf_op jit(solution)/shard_map/reduce_scatter | solution.py:245
  1038.0 26.3 %reduce-scatter.20.cloned.1.call-done = bf16[512,256]{1,0:T(8,128)(2,1)} async-done(((bf16[2048,256]{1,0:T(8,128)(2,1)}), bf16[512,256]{1,0:T(8,128)(2,1)}) %reduce-scatter.20.cloned.1.call-update) | async-done | bytes 262160 | tf_op jit(solution)/shard_map/reduce_scatter | solution.py:242
  1066.1 57.1 %reduce-scatter.18.cloned.1.call-done = bf16[160,2048]{1,0:T(8,128)(2,1)} async-done(((bf16[1280,2048]{1,0:T(8,128)(2,1)}), bf16[160,2048]{1,0:T(8,128)(2,1)}) %reduce-scatter.18.cloned.1.call-update) | async-done | bytes 655376 | tf_op jit(solution)/shard_map/reduce_scatter | solution.py:235
  1124.7 39.8 %all-reduce = (f32[2048]{0:T(1024)}, f32[2048]{0:T(1024)}) all-reduce(f32[2048]{0:T(1024)S(1)} %get-tuple-element.54, f32[2048]{0:T(1024)S(1)} %get-tuple-element.52), channel_id=1, replica_groups=mesh['fsdp'=4,'tensor'=8] {'fsdp','tensor'}, use_global_device_ids=true, to_apply=%region_14.15 | all-reduce | flops 4096 | bytes 32768 | tf_op jit(solution)/shard_map/psum | solution.py:240
  1164.4 19.3 %reduce-scatter.14.cloned.1.call-done = bf16[160,2048]{1,0:T(8,128)(2,1)} async-done(((bf16[1280,2048]{1,0:T(8,128)(2,1)}), bf16[160,2048]{1,0:T(8,128)(2,1)}) %reduce-scatter.14.cloned.1.call-update) | async-done | bytes 655376 | tf_op jit(solution)/shard_map/reduce_scatter | solution.py:190
  (186 shorter events, 262.7 us)
Async XLA Ops:
  7.2 33.1 %all-gather.17.cloned.1.call-start = ((), (), s32[]{:S(2)}) async-start(), calls=%async_computation.14 | async-start | bytes 1310720 | tf_op jit(solution)/shard_map/all_gather | solution.py:148
  7.9 75.4 %all-gather.11.cloned.1.call-start = ((), (), s32[]{:S(2)}) async-start(), calls=%async_computation.11 | async-start | bytes 5898240 | tf_op jit(solution)/shard_map/all_gather | solution.py:167
  12.7 100.2 %all-gather.15.cloned.1.call-start = ((), (), s32[]{:S(2)}) async-start(), calls=%async_computation.13 | async-start | bytes 1310720 | tf_op jit(solution)/shard_map/all_gather | solution.py:147
  13.4 128.3 %all-gather.13.cloned.1.call-start = ((), (), s32[]{:S(2)}) async-start(), calls=%async_computation.12 | async-start | bytes 1310720 | tf_op jit(solution)/shard_map/all_gather | solution.py:149
  14.0 156.6 %all-gather.19.cloned.1.call-start = ((), (), s32[]{:S(2)}) async-start(), calls=%async_computation.15 | async-start | bytes 1310720 | tf_op jit(solution)/shard_map/all_gather | solution.py:150
  14.6 243.9 %reduce-scatter.12.cloned.1.call-start = ((), (), s32[]{:S(2)}) async-start(), calls=%async_computation.16 | async-start | bytes 11796480 | tf_op jit(solution)/shard_map/reduce_scatter | solution.py:177
  177.4 196.3 %all-gather.25.cloned.1.call-start = ((), (), s32[]{:S(2)}) async-start(), calls=%async_computation.19 | async-start | bytes 5242880 | tf_op jit(solution)/shard_map/all_gather | solution.py:152
  178.1 211.2 %all-gather.21.cloned.1.call-start = ((), (), s32[]{:S(2)}) async-start(), calls=%async_computation.17 | async-start | bytes 5898240 | tf_op jit(solution)/shard_map/all_gather | solution.py:184
  261.2 210.5 %all-gather.23.cloned.1.call-start = ((), (), s32[]{:S(2)}) async-start(), calls=%async_computation.18 | async-start | bytes 5242880 | tf_op jit(solution)/shard_map/all_gather | solution.py:151
  261.9 290.5 %all-gather.27.cloned.1.call-start = ((), (), s32[]{:S(2)}) async-start(), calls=%async_computation.20 | async-start | bytes 5242880 | tf_op jit(solution)/shard_map/all_gather | solution.py:153
  262.0 2.2 collective-permute-start
  266.2 31.1 %collective-permute-start.1 = (bf16[2,160,2048]{2,1,0:T(8,128)(2,1)}, bf16[2,160,2048]{2,1,0:T(8,128)(2,1)}, u32[]{:S(2)}, u32[]{:S(2)}) collective-permute-start(bf16[2,160,2048]{2,1,0:T(8,128)(2,1)} %get-tuple-element.84), channel_id=1, source_target_pairs={{0,2},{1,3},{2,0},{3,1},{4,6},{5,7},{6,4},{7,5},{8,10},{9,11},{10,... | collective-permute-start | bytes 3932168 | tf_op jit(solution)/shard_map/ppermute | solution.py:24
  267.6 399.0 %reduce-scatter.16.cloned.1.call-start = ((), (), s32[]{:S(2)}) async-start(), calls=%async_computation.22 | async-start | bytes 11796480 | tf_op jit(solution)/shard_map/reduce_scatter | solution.py:212
  301.4 65.4 %collective-permute-start.2 = (bf16[4,160,2048]{2,1,0:T(8,128)(2,1)}, bf16[4,160,2048]{2,1,0:T(8,128)(2,1)}, u32[]{:S(2)}, u32[]{:S(2)}) collective-permute-start(bf16[4,160,2048]{2,1,0:T(8,128)(2,1)} %bitcast.18), channel_id=1, source_target_pairs={{0,4},{1,5},{2,6},{3,7},{4,0},{5,1},{6,2},{7,3},{8,12},{9,13},{10,... | collective-permute-start | bytes 7864328 | tf_op jit(solution)/shard_map/ppermute | solution.py:24
  586.3 125.8 %all-gather.29.cloned.1.call-start = ((), (), s32[]{:S(2)}) async-start(), calls=%async_computation.23 | async-start | bytes 5898240 | tf_op jit(solution)/shard_map/all_gather | solution.py:218
  670.9 157.5 %reduce-scatter.32.cloned.1.call-start = ((), (), s32[]{:S(2)}) async-start(), calls=%async_computation.31 | async-start | bytes 5242880 | tf_op jit(solution)/shard_map/reduce_scatter | solution.py:260
  681.0 189.7 %reduce-scatter.30.cloned.1.call-start = ((), (), s32[]{:S(2)}) async-start(), calls=%async_computation.30 | async-start | bytes 5242880 | tf_op jit(solution)/shard_map/reduce_scatter | solution.py:257
  691.3 258.9 %reduce-scatter.28.cloned.1.call-start = ((), (), s32[]{:S(2)}) async-start(), calls=%async_computation.29 | async-start | bytes 5242880 | tf_op jit(solution)/shard_map/reduce_scatter | solution.py:254
  701.5 278.6 %reduce-scatter.26.cloned.1.call-start = ((), (), s32[]{:S(2)}) async-start(), calls=%async_computation.28 | async-start | bytes 1310720 | tf_op jit(solution)/shard_map/reduce_scatter | solution.py:251
  717.1 291.0 %reduce-scatter.24.cloned.1.call-start = ((), (), s32[]{:S(2)}) async-start(), calls=%async_computation.27 | async-start | bytes 1310720 | tf_op jit(solution)/shard_map/reduce_scatter | solution.py:248
  753.8 282.4 %reduce-scatter.22.cloned.1.call-start = ((), (), s32[]{:S(2)}) async-start(), calls=%async_computation.26 | async-start | bytes 1310720 | tf_op jit(solution)/shard_map/reduce_scatter | solution.py:245
  795.9 268.3 %reduce-scatter.20.cloned.1.call-start = ((), (), s32[]{:S(2)}) async-start(), calls=%async_computation.25 | async-start | bytes 1310720 | tf_op jit(solution)/shard_map/reduce_scatter | solution.py:242
  801.1 322.1 %reduce-scatter.18.cloned.1.call-start = ((), (), s32[]{:S(2)}) async-start(), calls=%async_computation.24 | async-start | bytes 5898240 | tf_op jit(solution)/shard_map/reduce_scatter | solution.py:235
  818.3 365.5 %reduce-scatter.14.cloned.1.call-start = ((), (), s32[]{:S(2)}) async-start(), calls=%async_computation.21 | async-start | bytes 5898240 | tf_op jit(solution)/shard_map/reduce_scatter | solution.py:190
  (33 other events, 1696.3 us)
Sparse Core Ops, SparseCore 0:
  9.6 30.6 all-gather.16
  42.8 40.5 all-gather.10
  84.9 27.9 all-gather.14
  114.3 27.4 all-gather.12
  143.2 27.4 all-gather.18
  177.5 81.0 reduce-scatter.11
  260.1 80.7 all-gather.24
  343.3 45.9 all-gather.20
  390.9 80.7 all-gather.22
  473.1 79.2 all-gather.26
  586.4 80.0 reduce-scatter.15
  671.0 41.0 all-gather.28
  714.4 76.7 reduce-scatter.31
  793.5 77.2 reduce-scatter.29
  872.9 77.2 reduce-scatter.27
  952.4 27.6 reduce-scatter.25
  982.3 25.7 reduce-scatter.23
  1010.3 25.8 reduce-scatter.21
  1038.5 25.7 reduce-scatter.19
  1067.9 55.2 reduce-scatter.17
  1126.6 57.1 reduce-scatter.13
